TPU v7x, 32 devices: a whole 2x2x4 slice. The times are simulated.
32 devices in a mesh: blk: 4 (over y, x), inner: 8 (over z, core).
Axes of the slice: x: 2, y: 2, z: 4, core: 2. Of those that a mesh axis runs over, the one named last changes fastest.
Arguments:
- points: float32 [4096, 128], P(('blk', 'inner')), may hold values from -8 to 8
- lengthscales: float32 [128], replicated, may hold values from 6 to 24
- noise_level: float32 [1], replicated, may hold values from 1 to 10
- iterate: float32 [4096, 64], P(('blk', 'inner')), may hold values from -6 to 6
- residual: float32 [4096, 64], P(('blk', 'inner')), may hold values from -6 to 6
- direction: float32 [4096, 64], P(('blk', 'inner')), may hold values from -6 to 6
Outputs:
- new_iterate: float32 [4096, 64], P(('blk', 'inner'))
- new_residual: float32 [4096, 64], P(('blk', 'inner'))
- new_direction: float32 [4096, 64], P(('blk', 'inner'))
All inputs are finite; a program needn't handle non-finite values.
Results may differ from a plain program's by a relative error of at most 0.00014.
Values sent between devices are 32-bit elements; how exact they have to be, the bound alone decides.
A program may use at most 64 MiB of HBM per device.

v0:
```python
import jax
import jax.numpy as jnp
from jax import lax
from jax.sharding import PartitionSpec as P


def from_behind(value, axis, by):
    size = lax.axis_size(axis)
    return lax.ppermute(value, axis, [(i, (i + by) % size) for i in range(size)])


def kernel_block(left, left_sq, right, right_sq):
    products = lax.dot_general(
        left,
        right,
        (((1,), (1,)), ((), ())),
        precision=lax.Precision.HIGHEST,
        preferred_element_type=jnp.float32,
    )
    return jnp.exp(-0.5 * (left_sq[:, None] + right_sq[None, :] - 2.0 * products))


def matmul(left, right):
    return jnp.dot(left, right, precision=lax.Precision.HIGHEST, preferred_element_type=jnp.float32)


def transposed(left, right):
    return lax.dot_general(
        left,
        right,
        (((0,), (0,)), ((), ())),
        precision=lax.Precision.HIGHEST,
        preferred_element_type=jnp.float32,
    )


def chol_solve(matrix, rhs_side):
    factor = jnp.linalg.cholesky(matrix)
    return jax.scipy.linalg.cho_solve((factor, True), rhs_side)


def on_device(points, lengthscales, noise_level, iterate, residual, direction):
    scaled = points / lengthscales[None, :]
    sq_norms = jnp.sum(scaled * scaled, axis=1)
    cycle_size = lax.axis_size("blk")
    group_pts, group_dir = (
        lax.all_gather(scaled, "inner", axis=0, tiled=True),
        lax.all_gather(direction, "inner", axis=0, tiled=True),
    )
    group_sq = jnp.sum(group_pts * group_pts, axis=1)
    partial_value = jnp.zeros((group_pts.shape[0], direction.shape[1]), jnp.float32)
    halfway = cycle_size // 2
    visitor = (scaled, sq_norms, direction, jnp.zeros_like(direction))
    returned = jnp.zeros_like(direction)
    for offset in range(halfway + 1):
        if offset > 0:
            visitor = from_behind((visitor[0], visitor[1], visitor[2], visitor[3]), "blk", 1)
        kernel_tile = kernel_block(group_pts, group_sq, visitor[0], visitor[1])
        partial_value = partial_value + matmul(kernel_tile, visitor[2])
        if 1 <= offset <= halfway - 1:
            carried = visitor[3] + transposed(kernel_tile, group_dir)
            visitor = (visitor[0], visitor[1], visitor[2], carried)
            if offset == halfway - 1:
                returned = from_behind(carried, "blk", -(halfway - 1))
    owned = lax.psum_scatter(partial_value, "inner", scatter_dimension=0, tiled=True)
    image = owned + returned + noise_level[0] * direction
    local_gram = transposed(direction, image)
    local_res = transposed(residual, residual)
    gram_raw, res_gram = lax.psum((local_gram, local_res), ("blk", "inner"))
    gram_matrix = 0.5 * (gram_raw + gram_raw.T)
    step_size = chol_solve(gram_matrix, res_gram)
    new_residual = residual - matmul(image, step_size)
    new_gram = lax.psum(transposed(new_residual, new_residual), ("blk", "inner"))
    new_iterate = iterate + matmul(direction, step_size)
    correction = chol_solve(res_gram, new_gram)
    new_direction = new_residual + matmul(direction, correction)
    return (new_iterate, new_residual, new_direction)


def solution(mesh):
    return jax.shard_map(
        on_device,
        mesh=mesh,
        in_specs=(
            P(("blk", "inner"), None),
            P(),
            P(),
            P(("blk", "inner"), None),
            P(("blk", "inner"), None),
            P(("blk", "inner"), None),
        ),
        out_specs=(P(("blk", "inner"), None), P(("blk", "inner"), None), P(("blk", "inner"), None)),
        check_vma=False,
    )
```

profile of v0, /device:TPU:0, one launch (start us, length us, event | category | flops | bytes accessed | tf_op | source)
XLA Modules:
  0.0 187.7 jit_solution(3288486812774204959)
XLA Ops:
  7.2 3.0 %collective-permute-start.6 = (f32[128,64]{0,1:T(8,128)S(1)}, f32[128,64]{0,1:T(8,128)S(1)}, u32[]{:S(2)}, u32[]{:S(2)}) collective-permute-start(f32[128,64]{0,1:T(8,128)S(1)} %broadcast_in_dim.2), channel_id=1, source_target_pairs={{0,8},{8,16},{16,24},{24,0},{1,9},{9,17},{17,25},{25,1},{2,10},{10... | collective-permute-start | bytes 98312 | tf_op jit(solution)/shard_map/ppermute | solution.py:9
  10.3 1.5 collective-permute-start.2
  11.8 0.9 multiply_reduce_fusion.1
  12.7 1.5 collective-permute-start
  14.3 0.6 collective-permute-start.1
  14.9 15.0 %all_gather.6 = f32[1024,128]{1,0:T(8,128)S(1)} all-gather(f32[128,128]{1,0:T(8,128)S(1)} %get-tuple-element.8), channel_id=1, replica_groups=mesh['blk'=4,'inner'=8] {'inner'}, dimensions={0}, use_global_device_ids=true | all-gather | bytes 589824 | tf_op jit(solution)/shard_map/all_gather | solution.py:47
  30.1 0.6 fusion.2
  30.7 0.7 fusion.34
  31.4 1.4 collective-permute-start.3
  32.8 1.5 collective-permute-start.5
  34.3 1.5 collective-permute-start.4
  36.4 0.9 convolution_add_fusion.1
  37.3 2.2 %collective-permute-done.4 = f32[128,128]{1,0:T(8,128)S(1)} collective-permute-done((f32[128,128]{1,0:T(8,128)S(1)}, f32[128,128]{1,0:T(8,128)S(1)}, u32[]{:S(2)}, u32[]{:S(2)}) %collective-permute-start.4) | collective-permute-done | bytes 65568 | tf_op jit(solution)/shard_map/ppermute | solution.py:9
  40.1 1.6 convolution_add_fusion
  41.7 14.3 %all_gather.7 = f32[1024,64]{0,1:T(8,128)S(1)} all-gather(f32[128,64]{0,1:T(8,128)S(1)} %copy-done), channel_id=1, replica_groups=mesh['blk'=4,'inner'=8] {'inner'}, dimensions={0}, use_global_device_ids=true | all-gather | bytes 294912 | tf_op jit(solution)/shard_map/all_gather | solution.py:48
  55.9 0.6 convolution_add_fusion.2
  56.5 0.8 collective-permute-start.7
  58.2 2.3 %collective-permute-done.7 = f32[128,64]{0,1:T(8,128)S(1)} collective-permute-done((f32[128,64]{0,1:T(8,128)S(1)}, f32[128,64]{0,1:T(8,128)S(1)}, u32[]{:S(2)}, u32[]{:S(2)}) %collective-permute-start.7) | collective-permute-done | bytes 32800 | tf_op jit(solution)/shard_map/ppermute | solution.py:9
  60.5 11.5 %reduce-scatter.2.cloned.1.call-done = f32[128,64]{0,1:T(8,128)} async-done(((f32[1024,64]{0,1:T(8,128)}), f32[128,64]{0,1:T(8,128)}) %reduce-scatter.2.cloned.1.call-update) | async-done | bytes 32784 | tf_op jit(solution)/shard_map/reduce_scatter | solution.py:65
  72.0 0.9 convolution_bitcast_fusion.2
  73.0 38.3 %all-reduce = (f32[64,64]{0,1:T(8,128)S(1)}, f32[64,64]{1,0:T(8,128)S(1)}) all-reduce(f32[64,64]{0,1:T(8,128)S(1)} %fusion.35, f32[64,64]{1,0:T(8,128)S(1)} %convolution_bitcast_fusion.2), channel_id=1, replica_groups=mesh['blk'=4,'inner'=8] {'blk','inner'}, use_global_device_ids=true, to_apply=%region_6.8 | all-reduce | flops 8192 | bytes 65536 | tf_op jit(solution)/shard_map/psum | solution.py:69
  111.5 5.8 %cholesky.44 = f32[64,64]{1,0:T(8,128)S(1)} custom-call(f32[64,64]{1,0:T(8,128)S(1)} %fusion.29), custom_call_target="Cholesky" | custom-call | tf_op jit(solution)/shard_map/jit(cholesky)/cholesky | solution.py:38
  117.3 0.6 compare_reduce_fusion.1
  118.0 0.7 fusion.18
  118.6 4.9 %custom-call.8 = f32[1,64,64]{1,2,0:T(8,128)S(1)} custom-call(f32[1,64,64]{2,1,0:T(8,128)S(1)} %fusion.18), custom_call_target="InvertDiagBlocksLowerTriangular" | custom-call | tf_op jit(solution)/shard_map/jit(_cho_solve)/triangular_solve | solution.py:39
  124.6 0.9 fusion.4
  125.9 41.5 %psum.23 = f32[64,64]{1,0:T(8,128)S(1)} all-reduce(f32[64,64]{1,0:T(8,128)S(1)} %fusion.36), channel_id=1, replica_groups=mesh['blk'=4,'inner'=8] {'blk','inner'}, use_global_device_ids=true, to_apply=%region_7.10 | all-reduce | flops 4096 | bytes 32768 | tf_op jit(solution)/shard_map/psum | solution.py:73
  167.5 5.8 %cholesky.55 = f32[64,64]{1,0:T(8,128)S(1)} custom-call(f32[64,64]{1,0:T(8,128)S(1)} %fusion.24), custom_call_target="Cholesky" | custom-call | tf_op jit(solution)/shard_map/jit(cholesky)/cholesky | solution.py:38
  173.4 0.6 compare_reduce_fusion
  174.0 0.7 fusion.19
  174.7 4.9 %custom-call.9 = f32[1,64,64]{1,2,0:T(8,128)S(1)} custom-call(f32[1,64,64]{2,1,0:T(8,128)S(1)} %fusion.19), custom_call_target="InvertDiagBlocksLowerTriangular" | custom-call | tf_op jit(solution)/shard_map/jit(_cho_solve)/triangular_solve | solution.py:39
  180.0 0.9 fusion.3
  (39 shorter events, 3.8 us)
Async XLA Ops:
  7.2 3.1 %copy-start = (f32[128,64]{0,1:T(8,128)S(1)}, f32[128,64]{0,1:T(8,128)}, u32[]{:S(2)}) copy-start(f32[128,64]{0,1:T(8,128)} %param.14) | copy-start | bytes 98308
  7.2 4.6 %copy-start.5 = (f32[128]{0:T(128)S(1)}, f32[128]{0:T(128)}, u32[]{:S(2)}) copy-start(f32[128]{0:T(128)} %param.10) | copy-start | bytes 1540
  7.2 64.8 %reduce-scatter.2.cloned.1.call-start = ((), (), s32[]{:S(2)}) async-start(), calls=%async_computation.1 | async-start | bytes 294912 | tf_op jit(solution)/shard_map/reduce_scatter | solution.py:65
  7.2 48.7 %collective-permute-start.6 = (f32[128,64]{0,1:T(8,128)S(1)}, f32[128,64]{0,1:T(8,128)S(1)}, u32[]{:S(2)}, u32[]{:S(2)}) collective-permute-start(f32[128,64]{0,1:T(8,128)S(1)} %broadcast_in_dim.2), channel_id=1, source_target_pairs={{0,8},{8,16},{16,24},{24,0},{1,9},{9,17},{17,25},{25,1},{2,10},{10... | collective-permute-start | bytes 98312 | tf_op jit(solution)/shard_map/ppermute | solution.py:9
  10.3 22.6 %collective-permute-start.2 = (f32[128,64]{0,1:T(8,128)S(1)}, f32[128,64]{0,1:T(8,128)S(1)}, u32[]{:S(2)}, u32[]{:S(2)}) collective-permute-start(f32[128,64]{0,1:T(8,128)S(1)} %copy-done), channel_id=1, source_target_pairs={{0,8},{8,16},{16,24},{24,0},{1,9},{9,17},{17,25},{25,1},{2,10},{10... | collective-permute-start | bytes 98312 | tf_op jit(solution)/shard_map/ppermute | solution.py:9
  12.7 18.7 %collective-permute-start = (f32[128]{0:T(128)S(1)}, f32[128]{0:T(128)S(1)}, u32[]{:S(2)}, u32[]{:S(2)}) collective-permute-start(f32[128]{0:T(128)S(1)} %get-tuple-element.7), channel_id=1, source_target_pairs={{0,8},{8,16},{16,24},{24,0},{1,9},{9,17},{17,25},{25,1},{2,10},{10... | collective-permute-start | bytes 1544 | tf_op jit(solution)/shard_map/ppermute | solution.py:9
  14.3 20.1 %collective-permute-start.1 = (f32[128,128]{1,0:T(8,128)S(1)}, f32[128,128]{1,0:T(8,128)S(1)}, u32[]{:S(2)}, u32[]{:S(2)}) collective-permute-start(f32[128,128]{1,0:T(8,128)S(1)} %get-tuple-element.8), channel_id=1, source_target_pairs={{0,8},{8,16},{16,24},{24,0},{1,9},{9,17},{17,25},{25,1},{2,10},{10... | collective-permute-start | bytes 196616 | tf_op jit(solution)/shard_map/ppermute | solution.py:9
  31.4 8.6 %collective-permute-start.3 = (f32[128]{0:T(128)S(1)}, f32[128]{0:T(128)S(1)}, u32[]{:S(2)}, u32[]{:S(2)}) collective-permute-start(f32[128]{0:T(128)S(1)} %collective-permute-done), channel_id=1, source_target_pairs={{0,8},{8,16},{16,24},{24,0},{1,9},{9,17},{17,25},{25,1},{2,10},{10... | collective-permute-start | bytes 1544 | tf_op jit(solution)/shard_map/ppermute | solution.py:9
  32.8 7.3 %collective-permute-start.5 = (f32[128,64]{0,1:T(8,128)S(1)}, f32[128,64]{0,1:T(8,128)S(1)}, u32[]{:S(2)}, u32[]{:S(2)}) collective-permute-start(f32[128,64]{0,1:T(8,128)S(1)} %collective-permute-done.2), channel_id=1, source_target_pairs={{0,8},{8,16},{16,24},{24,0},{1,9},{9,17},{17,25},{25,1},{2,10},{10... | collective-permute-start | bytes 98312 | tf_op jit(solution)/shard_map/ppermute | solution.py:9
  34.3 5.2 %collective-permute-start.4 = (f32[128,128]{1,0:T(8,128)S(1)}, f32[128,128]{1,0:T(8,128)S(1)}, u32[]{:S(2)}, u32[]{:S(2)}) collective-permute-start(f32[128,128]{1,0:T(8,128)S(1)} %collective-permute-done.1), channel_id=1, source_target_pairs={{0,8},{8,16},{16,24},{24,0},{1,9},{9,17},{17,25},{25,1},{2,10},{10... | collective-permute-start | bytes 196616 | tf_op jit(solution)/shard_map/ppermute | solution.py:9
  55.9 1.4 copy-start.2
  56.5 4.0 %collective-permute-start.7 = (f32[128,64]{0,1:T(8,128)S(1)}, f32[128,64]{0,1:T(8,128)S(1)}, u32[]{:S(2)}, u32[]{:S(2)}) collective-permute-start(f32[128,64]{0,1:T(8,128)S(1)} %convolution_add_fusion.2), channel_id=1, source_target_pairs={{0,24},{8,0},{16,8},{24,16},{1,25},{9,1},{17,9},{25,17},{2,26},{10... | collective-permute-start | bytes 98312 | tf_op jit(solution)/shard_map/ppermute | solution.py:9
  123.9 0.8 copy-start.4
  124.6 0.9 copy-start.3
  125.7 54.3 %copy-start.1 = (f32[128,64]{0,1:T(8,128)}, f32[128,64]{0,1:T(8,128)S(1)}, u32[]{:S(2)}) copy-start(f32[128,64]{0,1:T(8,128)S(1)} %convolution_subtract_fusion) | copy-start | bytes 98308
Sparse Core Ops, SparseCore 0:
  41.8 30.1 reduce-scatter.1
where the time goes:
time: 188 us
  blocking collectives  109 us (58%)
  other arithmetic  25.3 us (13%)
  waiting for transfers between devices  16.1 us (9%)
  between operations  14.9 us (8%)
  starting transfers between devices  11.9 us (6%)
  matrix products  9.55 us (5%)
    psum x1, blocking collectives, on_device(): lax.psum(transposed(new_residual, new_residual), ('blk', 'inner'))  41.5 us
    psum x1, blocking collectives, on_device(): gram_raw, res_gram = lax.psum((local_gram, local_res), ('blk', 'inner'))  38.3 us
    all_gather x1, blocking collectives, on_device(): lax.all_gather(scaled, 'inner', axis=0, tiled=True)  15 us
    all_gather x1, blocking collectives, on_device(): lax.all_gather(direction, 'inner', axis=0, tiled=True)  14.3 us
    another operation x6, other arithmetic, chol_solve(): factor = jnp.linalg.cholesky(matrix)  13 us
    ppermute x8, starting transfers between devices, from_behind(): lax.ppermute(value, axis, [(i, (i + by) % size) for i in range(size)])  11.8 us
    reduce_scatter x1, waiting for transfers between devices, on_device(): lax.psum_scatter(partial_value, 'inner', scatter_dimension=0, tiled=True)  11.5 us
    another operation x4, other arithmetic, chol_solve(): return jax.scipy.linalg.cho_solve((factor, True), rhs_side)  11.1 us
  transfers between devices with their start and end apart: 9, of which 3 were waited for; matrix products, arithmetic and copies ran while one was open for 4% of the time, Pallas kernels for 0%

commit v1 on v0

--- a/solution.py
+++ b/solution.py
@@ -70,7 +70,9 @@
     gram_matrix = 0.5 * (gram_raw + gram_raw.T)
     step_size = chol_solve(gram_matrix, res_gram)
     new_residual = residual - matmul(image, step_size)
-    new_gram = lax.psum(transposed(new_residual, new_residual), ("blk", "inner"))
+    new_gram = jnp.sum(
+        lax.all_gather(transposed(new_residual, new_residual), ("blk", "inner")), axis=0
+    )
     new_iterate = iterate + matmul(direction, step_size)
     correction = chol_solve(res_gram, new_gram)
     new_direction = new_residual + matmul(direction, correction)

time: 188 us -> 192 us (1.021)
  blocking collectives: 109 us -> 112 us
    all_gather x0 -> x1, blocking collectives: none -> 44.9 us  [on_device(): lax.all_gather(transposed(new_residual, new_residual), ('blk', 'inner'))]
    psum x1 -> x0, blocking collectives: 41.5 us -> none  [on_device(): lax.psum(transposed(new_residual, new_residual), ('blk', 'inner'))]
where the time goes in v1:
time: 192 us; the launch traced here: 191 us
  blocking collectives  112 us (58%)
  other arithmetic  25.4 us (13%)
  waiting for transfers between devices  16.2 us (8%)
  between operations  14.9 us (8%)
  starting transfers between devices  11.8 us (6%)
  matrix products  9.53 us (5%)
    all_gather x1, blocking collectives, on_device(): lax.all_gather(transposed(new_residual, new_residual), ('blk', 'inner'))  44.9 us
    psum x1, blocking collectives, on_device(): gram_raw, res_gram = lax.psum((local_gram, local_res), ('blk', 'inner'))  38.4 us
    all_gather x1, blocking collectives, on_device(): lax.all_gather(scaled, 'inner', axis=0, tiled=True)  15 us
    all_gather x1, blocking collectives, on_device(): lax.all_gather(direction, 'inner', axis=0, tiled=True)  14.2 us
    another operation x6, other arithmetic, chol_solve(): factor = jnp.linalg.cholesky(matrix)  13 us
    ppermute x8, starting transfers between devices, from_behind(): lax.ppermute(value, axis, [(i, (i + by) % size) for i in range(size)])  11.8 us
    reduce_scatter x1, waiting for transfers between devices, on_device(): lax.psum_scatter(partial_value, 'inner', scatter_dimension=0, tiled=True)  11.5 us
    another operation x4, other arithmetic, chol_solve(): return jax.scipy.linalg.cho_solve((factor, True), rhs_side)  11.1 us
  transfers between devices with their start and end apart: 9, of which 3 were waited for; matrix products, arithmetic and copies ran while one was open for 4% of the time, Pallas kernels for 0%

profile of v1, /device:TPU:0, one launch (start us, length us, event | category | flops | bytes accessed | tf_op | source)
XLA Modules:
  0.0 191.2 jit_solution(3578788799790931888)
XLA Ops:
  7.2 3.0 %collective-permute-start.6 = (f32[128,64]{0,1:T(8,128)S(1)}, f32[128,64]{0,1:T(8,128)S(1)}, u32[]{:S(2)}, u32[]{:S(2)}) collective-permute-start(f32[128,64]{0,1:T(8,128)S(1)} %broadcast_in_dim.2), channel_id=1, source_target_pairs={{0,8},{8,16},{16,24},{24,0},{1,9},{9,17},{17,25},{25,1},{2,10},{10... | collective-permute-start | bytes 98312 | tf_op jit(solution)/shard_map/ppermute | solution.py:9
  10.3 1.5 collective-permute-start.2
  11.8 0.9 multiply_reduce_fusion.1
  12.7 1.5 collective-permute-start
  14.3 0.6 collective-permute-start.1
  14.9 15.0 %all_gather.12 = f32[1024,128]{1,0:T(8,128)S(1)} all-gather(f32[128,128]{1,0:T(8,128)S(1)} %get-tuple-element.8), channel_id=1, replica_groups=mesh['blk'=4,'inner'=8] {'inner'}, dimensions={0}, use_global_device_ids=true | all-gather | bytes 589824 | tf_op jit(solution)/shard_map/all_gather | solution.py:47
  30.1 0.6 fusion.2
  30.7 0.7 fusion.34
  31.4 1.4 collective-permute-start.3
  32.8 1.5 collective-permute-start.5
  34.3 1.5 collective-permute-start.4
  36.4 0.9 convolution_add_fusion.1
  37.3 2.2 %collective-permute-done.4 = f32[128,128]{1,0:T(8,128)S(1)} collective-permute-done((f32[128,128]{1,0:T(8,128)S(1)}, f32[128,128]{1,0:T(8,128)S(1)}, u32[]{:S(2)}, u32[]{:S(2)}) %collective-permute-start.4) | collective-permute-done | bytes 65568 | tf_op jit(solution)/shard_map/ppermute | solution.py:9
  40.1 1.6 convolution_add_fusion
  41.7 14.2 %all_gather.13 = f32[1024,64]{0,1:T(8,128)S(1)} all-gather(f32[128,64]{0,1:T(8,128)S(1)} %copy-done), channel_id=1, replica_groups=mesh['blk'=4,'inner'=8] {'inner'}, dimensions={0}, use_global_device_ids=true | all-gather | bytes 294912 | tf_op jit(solution)/shard_map/all_gather | solution.py:48
  55.9 0.6 convolution_add_fusion.2
  56.5 0.7 collective-permute-start.7
  58.1 2.4 %collective-permute-done.7 = f32[128,64]{0,1:T(8,128)S(1)} collective-permute-done((f32[128,64]{0,1:T(8,128)S(1)}, f32[128,64]{0,1:T(8,128)S(1)}, u32[]{:S(2)}, u32[]{:S(2)}) %collective-permute-start.7) | collective-permute-done | bytes 32800 | tf_op jit(solution)/shard_map/ppermute | solution.py:9
  60.5 11.5 %reduce-scatter.2.cloned.1.call-done = f32[128,64]{0,1:T(8,128)} async-done(((f32[1024,64]{0,1:T(8,128)}), f32[128,64]{0,1:T(8,128)}) %reduce-scatter.2.cloned.1.call-update) | async-done | bytes 32784 | tf_op jit(solution)/shard_map/reduce_scatter | solution.py:65
  72.0 0.9 convolution_bitcast_fusion.2
  72.9 38.4 %all-reduce = (f32[64,64]{0,1:T(8,128)S(1)}, f32[64,64]{1,0:T(8,128)S(1)}) all-reduce(f32[64,64]{0,1:T(8,128)S(1)} %fusion.35, f32[64,64]{1,0:T(8,128)S(1)} %convolution_bitcast_fusion.2), channel_id=1, replica_groups=mesh['blk'=4,'inner'=8] {'blk','inner'}, use_global_device_ids=true, to_apply=%region_6.8 | all-reduce | flops 8192 | bytes 65536 | tf_op jit(solution)/shard_map/psum | solution.py:69
  111.5 5.8 %cholesky.44 = f32[64,64]{1,0:T(8,128)S(1)} custom-call(f32[64,64]{1,0:T(8,128)S(1)} %fusion.29), custom_call_target="Cholesky" | custom-call | tf_op jit(solution)/shard_map/jit(cholesky)/cholesky | solution.py:38
  117.4 0.6 compare_reduce_fusion.1
  118.0 0.7 fusion.18
  118.7 4.9 %custom-call.8 = f32[1,64,64]{1,2,0:T(8,128)S(1)} custom-call(f32[1,64,64]{2,1,0:T(8,128)S(1)} %fusion.18), custom_call_target="InvertDiagBlocksLowerTriangular" | custom-call | tf_op jit(solution)/shard_map/jit(_cho_solve)/triangular_solve | solution.py:39
  124.7 0.9 fusion.4
  126.0 5.8 %cholesky.55 = f32[64,64]{1,0:T(8,128)S(1)} custom-call(f32[64,64]{1,0:T(8,128)S(1)} %fusion.24), custom_call_target="Cholesky" | custom-call | tf_op jit(solution)/shard_map/jit(cholesky)/cholesky | solution.py:38
  131.9 0.6 compare_reduce_fusion
  132.5 0.7 fusion.19
  133.2 4.9 %custom-call.9 = f32[1,64,64]{1,2,0:T(8,128)S(1)} custom-call(f32[1,64,64]{2,1,0:T(8,128)S(1)} %fusion.19), custom_call_target="InvertDiagBlocksLowerTriangular" | custom-call | tf_op jit(solution)/shard_map/jit(_cho_solve)/triangular_solve | solution.py:39
  138.1 44.9 %all-gather = f32[2048,64]{1,0:T(8,128)S(1)} all-gather(f32[64,64]{1,0:T(8,128)S(1)} %fusion.36), channel_id=2, replica_groups=mesh['blk'=4,'inner'=8] {'blk','inner'}, dimensions={0}, use_global_device_ids=true | all-gather | bytes 540672 | tf_op jit(solution)/shard_map/all_gather | solution.py:74
  183.5 0.9 fusion.3
  (40 shorter events, 3.9 us)
Async XLA Ops:
  7.2 3.1 %copy-start = (f32[128,64]{0,1:T(8,128)S(1)}, f32[128,64]{0,1:T(8,128)}, u32[]{:S(2)}) copy-start(f32[128,64]{0,1:T(8,128)} %param.14) | copy-start | bytes 98308
  7.2 4.6 %copy-start.5 = (f32[128]{0:T(128)S(1)}, f32[128]{0:T(128)}, u32[]{:S(2)}) copy-start(f32[128]{0:T(128)} %param.10) | copy-start | bytes 1540
  7.2 64.8 %reduce-scatter.2.cloned.1.call-start = ((), (), s32[]{:S(2)}) async-start(), calls=%async_computation.1 | async-start | bytes 294912 | tf_op jit(solution)/shard_map/reduce_scatter | solution.py:65
  7.2 48.7 %collective-permute-start.6 = (f32[128,64]{0,1:T(8,128)S(1)}, f32[128,64]{0,1:T(8,128)S(1)}, u32[]{:S(2)}, u32[]{:S(2)}) collective-permute-start(f32[128,64]{0,1:T(8,128)S(1)} %broadcast_in_dim.2), channel_id=1, source_target_pairs={{0,8},{8,16},{16,24},{24,0},{1,9},{9,17},{17,25},{25,1},{2,10},{10... | collective-permute-start | bytes 98312 | tf_op jit(solution)/shard_map/ppermute | solution.py:9
  10.3 22.6 %collective-permute-start.2 = (f32[128,64]{0,1:T(8,128)S(1)}, f32[128,64]{0,1:T(8,128)S(1)}, u32[]{:S(2)}, u32[]{:S(2)}) collective-permute-start(f32[128,64]{0,1:T(8,128)S(1)} %copy-done), channel_id=1, source_target_pairs={{0,8},{8,16},{16,24},{24,0},{1,9},{9,17},{17,25},{25,1},{2,10},{10... | collective-permute-start | bytes 98312 | tf_op jit(solution)/shard_map/ppermute | solution.py:9
  12.7 18.7 %collective-permute-start = (f32[128]{0:T(128)S(1)}, f32[128]{0:T(128)S(1)}, u32[]{:S(2)}, u32[]{:S(2)}) collective-permute-start(f32[128]{0:T(128)S(1)} %get-tuple-element.7), channel_id=1, source_target_pairs={{0,8},{8,16},{16,24},{24,0},{1,9},{9,17},{17,25},{25,1},{2,10},{10... | collective-permute-start | bytes 1544 | tf_op jit(solution)/shard_map/ppermute | solution.py:9
  14.3 20.1 %collective-permute-start.1 = (f32[128,128]{1,0:T(8,128)S(1)}, f32[128,128]{1,0:T(8,128)S(1)}, u32[]{:S(2)}, u32[]{:S(2)}) collective-permute-start(f32[128,128]{1,0:T(8,128)S(1)} %get-tuple-element.8), channel_id=1, source_target_pairs={{0,8},{8,16},{16,24},{24,0},{1,9},{9,17},{17,25},{25,1},{2,10},{10... | collective-permute-start | bytes 196616 | tf_op jit(solution)/shard_map/ppermute | solution.py:9
  31.4 8.7 %collective-permute-start.3 = (f32[128]{0:T(128)S(1)}, f32[128]{0:T(128)S(1)}, u32[]{:S(2)}, u32[]{:S(2)}) collective-permute-start(f32[128]{0:T(128)S(1)} %collective-permute-done), channel_id=1, source_target_pairs={{0,8},{8,16},{16,24},{24,0},{1,9},{9,17},{17,25},{25,1},{2,10},{10... | collective-permute-start | bytes 1544 | tf_op jit(solution)/shard_map/ppermute | solution.py:9
  32.8 7.3 %collective-permute-start.5 = (f32[128,64]{0,1:T(8,128)S(1)}, f32[128,64]{0,1:T(8,128)S(1)}, u32[]{:S(2)}, u32[]{:S(2)}) collective-permute-start(f32[128,64]{0,1:T(8,128)S(1)} %collective-permute-done.2), channel_id=1, source_target_pairs={{0,8},{8,16},{16,24},{24,0},{1,9},{9,17},{17,25},{25,1},{2,10},{10... | collective-permute-start | bytes 98312 | tf_op jit(solution)/shard_map/ppermute | solution.py:9
  34.3 5.2 %collective-permute-start.4 = (f32[128,128]{1,0:T(8,128)S(1)}, f32[128,128]{1,0:T(8,128)S(1)}, u32[]{:S(2)}, u32[]{:S(2)}) collective-permute-start(f32[128,128]{1,0:T(8,128)S(1)} %collective-permute-done.1), channel_id=1, source_target_pairs={{0,8},{8,16},{16,24},{24,0},{1,9},{9,17},{17,25},{25,1},{2,10},{10... | collective-permute-start | bytes 196616 | tf_op jit(solution)/shard_map/ppermute | solution.py:9
  55.9 1.3 copy-start.2
  56.5 4.0 %collective-permute-start.7 = (f32[128,64]{0,1:T(8,128)S(1)}, f32[128,64]{0,1:T(8,128)S(1)}, u32[]{:S(2)}, u32[]{:S(2)}) collective-permute-start(f32[128,64]{0,1:T(8,128)S(1)} %convolution_add_fusion.2), channel_id=1, source_target_pairs={{0,24},{8,0},{16,8},{24,16},{1,25},{9,1},{17,9},{25,17},{2,26},{10... | collective-permute-start | bytes 98312 | tf_op jit(solution)/shard_map/ppermute | solution.py:9
  123.9 0.8 copy-start.4
  124.7 0.9 copy-start.3
  125.8 57.7 %copy-start.1 = (f32[128,64]{0,1:T(8,128)}, f32[128,64]{0,1:T(8,128)S(1)}, u32[]{:S(2)}) copy-start(f32[128,64]{0,1:T(8,128)S(1)} %convolution_subtract_fusion) | copy-start | bytes 98308
Sparse Core Ops, SparseCore 0:
  41.8 30.1 reduce-scatter.1
